TPU v7x, 512 devices: a whole 4x8x8 slice. The times are simulated.
512 devices in a mesh: row: 32 (over y, x), col: 16 (over z, core).
Axes of the slice: x: 4, y: 8, z: 8, core: 2. Of those that a mesh axis runs over, the one named last changes fastest.
Arguments:
- draws: bfloat16 [128, 65536], P('row', 'col'), may hold values from -6 to 6
- u_factors: bfloat16 [64, 64, 1024, 64], P('row', 'col'), may hold values from -0.09375 to 0.09375
- v_factors: bfloat16 [64, 64, 1024, 64], P('row', 'col'), may hold values from -0.1875 to 0.1875
- ranks: int32 [64, 64], P('row', 'col'), may hold values from 16 to 64
- near: int32 [64, 16], P('row'), may hold values from 0 to 63, as said below
- row_coords: float32 [2, 65536], P(None, 'row'), may hold values from 0 to 16
- col_coords: float32 [2, 65536], replicated, may hold values from 0 to 16
Outputs:
- applied: float32 [128, 65536], P('col', 'row')
Inputs may be any that keep to these rules, and one draw needn't show every extreme that they name: `ranks`: the rank of a tile; factor columns from its rank on are padding. `near`: each block row lists 16 different block columns.
All inputs are finite; a program needn't handle non-finite values.
Results may differ from a plain program's by a relative error of at most 0.0029.
Values may be sent and summed in bfloat16 or wider, within the bound.
No kernel may reach another device: no remote copies, remote signals or barrier semaphores. Data moves between devices by JAX's collectives and lax.ppermute only.
A program may use at most 64 MiB of HBM per device.

v0:
```python
import jax
import jax.numpy as jnp
from jax import lax
from jax.sharding import PartitionSpec as P


def matern_tile(col_part, row_part):
    delta_x = col_part[0][:, None] - row_part[0][None, :]
    delta_y = col_part[1][:, None] - row_part[1][None, :]
    kernel = jnp.exp(-jnp.sqrt(delta_x * delta_x + delta_y * delta_y)) * 0.03125
    return kernel.astype(jnp.bfloat16)


def per_device(draws, u_factors, v_factors, ranks, near, row_coords, col_coords):
    rows_local, cols_local, tile, rank = u_factors.shape
    first_col = lax.axis_index("col") * cols_local
    whole = lax.all_gather(draws, "row", axis=0, tiled=True)
    width = whole.shape[0]
    column_ids = first_col + jnp.arange(cols_local, dtype=jnp.int32)
    flagged = jnp.any(near[:, :, None] == column_ids[None, None, :], axis=1)
    keep = (jnp.arange(rank, dtype=jnp.int32)[None, None, :] < ranks[:, :, None]) & jnp.logical_not(
        flagged
    )[:, :, None]
    blocks = whole.reshape(width, cols_local, tile)
    reduced = jnp.einsum("nbt,abtk->nabk", blocks, v_factors, preferred_element_type=jnp.float32)
    reduced = jnp.where(keep[None], reduced, 0.0).astype(jnp.bfloat16)
    partial_value = jnp.einsum(
        "nabk,abtk->nat", reduced, u_factors, preferred_element_type=jnp.float32
    )
    partial_value = partial_value.reshape(width, rows_local * tile)
    local_cols = lax.dynamic_slice_in_dim(col_coords, first_col * tile, cols_local * tile, 1)

    def add_tile(step, total):
        row_pos = step // cols_local
        col_pos = step % cols_local

        def dense(acc):
            tile_matrix = matern_tile(
                lax.dynamic_slice_in_dim(local_cols, col_pos * tile, tile, 1),
                lax.dynamic_slice_in_dim(row_coords, row_pos * tile, tile, 1),
            )
            piece = lax.dynamic_slice_in_dim(whole, col_pos * tile, tile, 1)
            product = jnp.dot(piece, tile_matrix, preferred_element_type=jnp.float32)
            current = lax.dynamic_slice_in_dim(acc, row_pos * tile, tile, 1)
            return lax.dynamic_update_slice_in_dim(acc, current + product, row_pos * tile, 1)

        return lax.cond(flagged[row_pos, col_pos], dense, lambda acc: acc, total)

    partial_value = lax.fori_loop(0, rows_local * cols_local, add_tile, partial_value)
    result = lax.psum_scatter(partial_value, "col", scatter_dimension=0, tiled=True)
    return result


def solution(mesh):
    return jax.shard_map(
        per_device,
        mesh=mesh,
        in_specs=(
            P("row", "col"),
            P("row", "col", None, None),
            P("row", "col", None, None),
            P("row", "col"),
            P("row", None),
            P(None, "row"),
            P(),
        ),
        out_specs=P("col", "row"),
        check_vma=False,
    )
```

profile of v0, /device:TPU:6, one launch (start us, length us, event | category | flops | bytes accessed | tf_op | source)
XLA Modules:
  0.0 207.3 jit_solution(1373862873125441184)
XLA Ops:
  6.5 0.0 copy-start
  6.5 0.0 all-gather.3.cloned.1.call-start
  6.5 0.7 all-gather.3.cloned.1.call-update
  7.3 0.0 reduce-scatter.2.cloned.1.call-start
  7.3 0.9 compare_reduce_fusion
  8.2 0.8 fusion.14
  9.0 0.8 constant_dynamic-slice_fusion.2
  9.7 85.8 %all-gather.3.cloned.1.call-done = bf16[32,4,4096]{2,1,0:T(4,128)(2,1)} async-done(((bf16[1,4,4096]{2,1,0:T(4,128)(2,1)}), bf16[32,4,4096]{2,1,0:T(4,128)(2,1)}) %all-gather.3.cloned.1.call-update) | async-done | bytes 1048592 | tf_op jit(solution)/shard_map/all_gather | solution.py:17
  95.5 1.9 reshape.23
  97.4 0.0 copy-done
  97.4 2.2 %convolution_bitcast_fusion = f32[128,2,1024]{2,0,1:T(8,128)S(1)} fusion(bf16[2,4,1024,64]{2,3,1,0:T(8,128)(2,1)S(1)} %copy-done, bf16[2,4,1024,64]{2,3,1,0:T(8,128)(2,1)} %param.13, bf16[128,4,1024]{2,1,0:T(4,128)(2,1)S(1)} %reshape.23, pred[2,4,64]{2,1,0:T(4,128)(4,1)S(1)} %fusion.14), kind=kOutput, calls=%fused_computation.9 | convolution fusion | flops 268566528 | bytes 4194816 | tf_op jit(solution)/shard_map/nabk,abtk->nat/dot_general | solution.py:27
  99.6 1.4 copy.16
  100.9 0.0 copy-start.1
  100.9 1.6 copy.17
  102.6 0.0 copy-done.1
  102.6 0.0 copy-start.3
  102.6 1.1 reshape.27
  103.7 0.0 copy-done.3
  103.7 9.6 %while.18 = (s32[]{:T(128)}, f32[128,2048]{1,0:T(8,128)S(1)}, pred[2,4]{1,0:T(4,128)(4,1)S(1)}, bf16[128,4096]{1,0:T(8,128)(2,1)}, f32[2,4096]{1,0:T(2,128)S(1)}...) while((s32[]{:T(128)}, f32[128,2048]{1,0:T(8,128)S(1)}, ...), condition=%wide.region_4.5_spmd, body=%wide.region_1.4_spmd.sunk | while | flops 276955168 | bytes 1360371 | solution.py:49
  103.7 0.6 dynamic_slice.31
  104.9 0.6 dynamic_slice.31
  106.1 0.6 dynamic_slice.31
  107.3 0.6 dynamic_slice.31
  108.5 0.6 dynamic_slice.31
  109.8 0.6 dynamic_slice.31
  111.0 0.6 dynamic_slice.31
  112.2 0.6 dynamic_slice.31
  113.3 0.0 copy-start.2
  113.4 1.0 copy-done.2
  114.3 0.0 reduce-scatter.2.cloned.1.call-update
  114.3 86.2 %reduce-scatter.2.cloned.1.call-done = f32[8,2048]{1,0:T(8,128)} async-done(((f32[128,2048]{1,0:T(8,128)}), f32[8,2048]{1,0:T(8,128)}) %reduce-scatter.2.cloned.1.call-update) | async-done | bytes 65552 | tf_op jit(solution)/shard_map/reduce_scatter | solution.py:50
  (10 shorter events, 0.1 us)
Async XLA Ops:
  6.5 90.8 %copy-start = (bf16[2,4,1024,64]{2,3,1,0:T(8,128)(2,1)S(1)}, bf16[2,4,1024,64]{2,3,1,0:T(8,128)(2,1)}, u32[]{:S(2)}) copy-start(bf16[2,4,1024,64]{2,3,1,0:T(8,128)(2,1)} %param.12) | copy-start | bytes 3145732
  6.5 89.0 %all-gather.3.cloned.1.call-start = ((), (), s32[]{:S(2)}) async-start(), calls=%async_computation.2 | async-start | bytes 1081344 | tf_op jit(solution)/shard_map/all_gather | solution.py:17
  7.3 193.2 %reduce-scatter.2.cloned.1.call-start = ((), (), s32[]{:S(2)}) async-start(), calls=%async_computation.1 | async-start | bytes 1114112 | tf_op jit(solution)/shard_map/reduce_scatter | solution.py:50
  100.9 1.7 copy-start.1
  102.6 1.1 copy-start.3
  113.3 1.0 copy-start.2
Sparse Core Ops, SparseCore 0:
  10.5 84.9 all-gather.2
  114.5 86.0 reduce-scatter.1
where the time goes:
time: 208 us; the launch traced here: 207 us
  waiting for transfers between devices  173 us (83%)
  between operations  13.5 us (6%)
  local copies, waits for them, and re-layouts  12.4 us (6%)
  loops' own time  4.97 us (2%)
  matrix products  2.19 us (1%)
    reduce_scatter x1, waiting for transfers between devices, per_device(): lax.psum_scatter(partial_value, 'col', scatter_dimension=0, tiled=True)  86.2 us
    all_gather x1, waiting for transfers between devices, per_device(): whole = lax.all_gather(draws, 'row', axis=0, tiled=True)  85.8 us
    another operation x1, loops' own time, per_device(): lax.fori_loop(0, rows_local * cols_local, add_tile, partial_value)  4.87 us
    dynamic_slice x8, local copies, waits for them, and re-layouts, add_tile(): return lax.cond(flagged[row_pos, col_pos], dense, lambda acc: acc, total)  4.64 us
  transfers between devices with their start and end apart: 2, of which 2 were waited for; matrix products, arithmetic and copies ran while one was open for 1% of the time, Pallas kernels for 0%

commit v1 on v0

v1 whole, which is shorter than its diff:
```python
import functools

import jax
import jax.numpy as jnp
from jax import lax
from jax.experimental import pallas as pl
from jax.experimental.pallas import tpu as pltpu
from jax.sharding import Mesh, PartitionSpec as P

LOG2E = 1.4426950408889634
AXES = ("y", "x", "z", "c")
SIZES = (8, 4, 8, 2)
VMEM = pltpu.MemorySpace.VMEM
SMEM = pltpu.MemorySpace.SMEM
HBM = pltpu.MemorySpace.HBM


def first_column(cols_local):
    return (lax.axis_index("z") * 2 + lax.axis_index("c")) * cols_local


def is_near(near_ref, row, column):
    hit = near_ref[row, 0] == column
    for slot in range(1, near_ref.shape[1]):
        hit = jnp.logical_or(hit, near_ref[row, slot] == column)
    return hit


def dense_kernel(near_ref, row_ref, col_hbm, out_hbm, coords, wide_x, wide_y, block, todo, sem, out_sems):
    rows_local, cols_local, tile, _ = out_hbm.shape
    first = first_column(cols_local)
    start = pl.multiple_of(first * tile, tile)
    fetch = pltpu.make_async_copy(col_hbm.at[:, pl.ds(start, cols_local * tile)], coords, sem)
    fetch.start()
    count = jnp.int32(0)
    for b in range(cols_local):
        for a in range(rows_local):
            todo[count] = b * rows_local + a
            count = count + is_near(near_ref, a, first + b).astype(jnp.int32)
    fetch.wait()
    step = 32

    def store(index):
        a, b, slot = lax.rem(todo[index], rows_local), lax.div(todo[index], rows_local), lax.rem(index, 2)
        return pltpu.make_async_copy(block.at[slot], out_hbm.at[a, b], out_sems.at[slot])

    def make_tile(index, carry):
        a, b, slot = lax.rem(todo[index], rows_local), lax.div(todo[index], rows_local), lax.rem(index, 2)

        @pl.when(index >= 2)
        def _():
            store(index - 2).wait()

        for part in range(tile // 128):
            at = pl.multiple_of(b * tile + part * 128, 128)
            for axis, wide in ((0, wide_x), (1, wide_y)):
                line = coords[axis : axis + 1, pl.ds(at, 128)] * LOG2E
                wide[part * 128 : (part + 1) * 128, :] = jnp.broadcast_to(line, (128, 128)).T
        row_at = pl.multiple_of(a * tile, tile)
        line_x = row_ref[0:1, pl.ds(row_at, tile)] * LOG2E
        line_y = row_ref[1:2, pl.ds(row_at, tile)] * LOG2E

        def body(k, carry):
            at = pl.multiple_of(k * step, step)
            col_x = wide_x[pl.ds(at, step), :]
            col_y = wide_y[pl.ds(at, step), :]
            for part in range(tile // 128):
                lanes = slice(part * 128, (part + 1) * 128)
                dx = col_x - line_x[:, lanes]
                dy = col_y - line_y[:, lanes]
                square = dx * dx + dy * dy
                dist = square * lax.rsqrt(jnp.maximum(square, 1e-35))
                block[slot, pl.ds(at, step), lanes] = jnp.exp2(-dist).astype(jnp.bfloat16)
            return carry

        lax.fori_loop(0, tile // step, body, 0)
        store(index).start()
        return carry

    lax.fori_loop(0, count, make_tile, 0)
    for back in (2, 1):

        @pl.when(count >= back)
        def _(back=back):
            store(count - back).wait()


def dense_tiles(near, row_coords, col_coords, rows_local, cols_local, tile):
    return pl.pallas_call(
        dense_kernel,
        out_shape=jax.ShapeDtypeStruct((rows_local, cols_local, tile, tile), jnp.bfloat16),
        in_specs=[
            pl.BlockSpec(memory_space=SMEM),
            pl.BlockSpec(memory_space=VMEM),
            pl.BlockSpec(memory_space=HBM),
        ],
        out_specs=pl.BlockSpec(memory_space=HBM),
        scratch_shapes=[
            pltpu.VMEM((2, cols_local * tile), jnp.float32),
            pltpu.VMEM((tile, 128), jnp.float32),
            pltpu.VMEM((tile, 128), jnp.float32),
            pltpu.VMEM((2, tile, tile), jnp.bfloat16),
            pltpu.SMEM((rows_local * cols_local + 1,), jnp.int32),
            pltpu.SemaphoreType.DMA,
            pltpu.SemaphoreType.DMA((2,)),
        ],
        compiler_params=pltpu.CompilerParams(vmem_limit_bytes=52 << 20),
        cost_estimate=pl.CostEstimate(flops=20_000_000, bytes_accessed=16_000_000, transcendentals=16_000_000),
        name="dense_tiles",
    )(near, row_coords, col_coords)


def apply_kernel(row, near_ref, ranks_ref, draws_ref, v_ref, u_ref, dense_hbm, keep_ref, send_ref, total, dense, sems):
    cols_local, rank, tile = v_ref.shape[1:]
    width = draws_ref.shape[0]
    half = width // 2
    first = first_column(cols_local)
    near = [is_near(near_ref, row, first + b) for b in range(cols_local)]
    fetches = [pltpu.make_async_copy(dense_hbm.at[row, b], dense.at[b], sems.at[b]) for b in range(cols_local)]
    for b in range(cols_local):

        @pl.when(near[b])
        def _(b=b):
            fetches[b].start()

    total[...] = jnp.zeros_like(total)
    for b in range(cols_local):
        lanes = slice(b * tile, (b + 1) * tile)

        @pl.when(near[b])
        def _(b=b, lanes=lanes):
            fetches[b].wait()
            piece = draws_ref[:, lanes]
            for at in range(0, tile, 256):
                part = slice(at, at + 256)
                product = jnp.dot(piece, dense[b, :, part], preferred_element_type=jnp.float32)
                total[:, part] += product * 0.03125

        @pl.when(jnp.logical_not(near[b]))
        def _(b=b, lanes=lanes):
            reduced = lax.dot_general(
                draws_ref[:, lanes], v_ref[row, b], (((1,), (1,)), ((), ())), preferred_element_type=jnp.float32
            )
            ids = lax.broadcasted_iota(jnp.int32, reduced.shape, 1)
            reduced = jnp.where(ids < ranks_ref[row, b], reduced, 0.0).astype(jnp.bfloat16)
            for at in range(0, tile, 256):
                part = slice(at, at + 256)
                total[:, part] += jnp.dot(reduced, u_ref[row, b, :, part], preferred_element_type=jnp.float32)

    core = lax.axis_index("c")
    keep_ref[...] = total[pl.ds(pl.multiple_of(core * half, half), half), :]
    send_ref[...] = total[pl.ds(pl.multiple_of((1 - core) * half, half), half), :]


def apply_row(row, near, ranks, draws, v_factors, u_factors, dense):
    cols_local, _, tile = v_factors.shape[1:]
    width = draws.shape[0]
    half = jax.ShapeDtypeStruct((width // 2, tile), jnp.float32)
    return pl.pallas_call(
        functools.partial(apply_kernel, row),
        out_shape=(half, half),
        in_specs=[pl.BlockSpec(memory_space=SMEM)] * 2
        + [pl.BlockSpec(memory_space=VMEM)] * 3
        + [pl.BlockSpec(memory_space=HBM)],
        out_specs=(pl.BlockSpec(memory_space=VMEM),) * 2,
        scratch_shapes=[
            pltpu.VMEM((width, tile), jnp.float32),
            pltpu.VMEM((cols_local, tile, tile), jnp.bfloat16),
            pltpu.SemaphoreType.DMA((cols_local,)),
        ],
        compiler_params=pltpu.CompilerParams(vmem_limit_bytes=52 << 20),
        cost_estimate=pl.CostEstimate(flops=500_000_000, bytes_accessed=8_000_000, transcendentals=0),
        name="apply_row",
    )(near, ranks, draws, v_factors, u_factors, dense)


def fold_kernel(*refs):
    *parts, out_ref = refs
    rows_local = len(parts) // 2
    tile = parts[0].shape[1]
    for row in range(rows_local):
        both = parts[row][...] + parts[rows_local + row][...]
        for z in range(out_ref.shape[0]):
            block = jnp.concatenate([both[4 * z : 4 * z + 4], both[32 + 4 * z : 36 + 4 * z]], axis=0)
            out_ref[z, :, row * tile : (row + 1) * tile] = block.astype(jnp.bfloat16)


def per_device(draws, u_factors, v_factors, ranks, near, row_coords, col_coords):
    rows_local, cols_local, tile, rank = u_factors.shape
    ny, nx, nz, nc = SIZES
    own = draws.shape[0]
    span = draws.shape[1]
    u_t = jnp.swapaxes(u_factors, 2, 3)
    v_t = jnp.swapaxes(v_factors, 2, 3)
    dense = dense_tiles(near, row_coords, col_coords, rows_local, cols_local, tile)
    column = lax.all_to_all(jnp.broadcast_to(draws[None], (ny, own, span)), "y", 0, 0)
    column = column.reshape(ny * own, span)
    plane = lax.all_to_all(jnp.broadcast_to(column[None], (nx, ny * own, span)), "x", 0, 0)
    plane = plane.reshape(nx * ny * own, span)
    keeps, others = [], []
    for row in range(rows_local):
        keep, send = apply_row(row, near, ranks, plane, v_t, u_t, dense)
        keeps.append(keep)
        pairs = [(i, i ^ 1) for i in range(nz * nc)]
        others.append(lax.ppermute(send, ("z", "c"), pairs))
    blocks = pl.pallas_call(
        fold_kernel,
        out_shape=jax.ShapeDtypeStruct((nz, 8, rows_local * tile), jnp.bfloat16),
        compiler_params=pltpu.CompilerParams(vmem_limit_bytes=6 << 20),
        name="fold",
    )(*keeps, *others)
    spread = lax.all_to_all(blocks, "z", 0, 0)
    return jnp.sum(spread.astype(jnp.float32), axis=0)


def solution(mesh):
    fine = Mesh(mesh.devices.reshape(SIZES), AXES)
    row, col = ("y", "x"), ("z", "c")
    return jax.shard_map(
        per_device,
        mesh=fine,
        in_specs=(
            P(row, col),
            P(row, col, None, None),
            P(row, col, None, None),
            P(row, col),
            P(row, None),
            P(None, row),
            P(),
        ),
        out_specs=P(col, row),
        check_vma=False,
    )
```

time: 208 us -> 86.9 us (0.42)
  the two profiles are of different devices: /device:TPU:6 before, /device:TPU:16 now
where the time goes in v1:
time: 86.9 us; the launch traced here: 86.2 us
  blocking collectives  53.8 us (62%)
  waiting for transfers between devices  10.8 us (12%)
  starting transfers between devices  8.29 us (10%)
  Pallas kernels  8.1 us (9%)
  local copies, waits for them, and re-layouts  4.42 us (5%)
    all_to_all x1, blocking collectives, per_device(): spread = lax.all_to_all(blocks, 'z', 0, 0)  37.3 us
    all_to_all x1, blocking collectives, per_device(): lax.all_to_all(jnp.broadcast_to(draws[None], (ny, own, span)), 'y', 0, 0)  16.5 us
    all_to_all x1, waiting for transfers between devices, per_device(): lax.all_to_all(jnp.broadcast_to(column[None], (nx, ny * own, span)), 'x',...  9.67 us
    pallas_call x2, Pallas kernels, apply_row(): pl.pallas_call(functools.partial(apply_kernel, row), out_shape=(half, hal...  7.27 us
    ppermute x2, starting transfers between devices, per_device(): others.append(lax.ppermute(send, ('z', 'c'), pairs))  4.33 us
    all_to_all x1, starting transfers between devices, per_device(): lax.all_to_all(jnp.broadcast_to(column[None], (nx, ny * own, span)), 'x',...  3.97 us
    unnamed x10, local copies, waits for them, and re-layouts  2.45 us
  transfers between devices with their start and end apart: 3, of which 2 were waited for; matrix products, arithmetic and copies ran while one was open for 0% of the time, Pallas kernels for 1%

profile of v1, /device:TPU:16, one launch (start us, length us, event | category | flops | bytes accessed | tf_op | source)
XLA Modules:
  0.0 86.2 jit_solution(15411348339381802450)
XLA Ops:
  0.0 0.8 broadcast_in_dim.6
  0.8 16.5 %all_to_all.15 = bf16[8,4,4096]{2,1,0:T(4,128)(2,1)S(1)} all-to-all(bf16[8,4,4096]{2,1,0:T(4,128)(2,1)S(1)} %broadcast_in_dim.6), channel_id=1, replica_groups=mesh['y'=8,'x'=4,'z'=8,'c'=2] {'y'}, dimensions={0} | all-to-all | bytes 524288 | tf_op jit(solution)/shard_map/all_to_all | solution.py:196
  17.4 0.1 broadcast_in_dim.14
  17.4 0.0 copy-start.1
  17.5 0.0 copy-start.2
  17.5 1.1 %broadcast_in_dim.15 = bf16[4,32,4096]{2,1,0:T(8,128)(2,1)} broadcast(bf16[32,4096]{1,0:T(8,128)(2,1)S(1)} %broadcast_in_dim.14), dimensions={1,2} | broadcast | bytes 1310720 | tf_op jit(solution)/shard_map/broadcast_in_dim | solution.py:198
  18.6 4.0 %all-to-all-start.1 = ((bf16[4,32,4096]{2,1,0:T(8,128)(2,1)}), bf16[4,32,4096]{2,1,0:T(8,128)(2,1)S(1)}, u32[]{:S(2)}, u32[]{:S(2)}) async-start(bf16[4,32,4096]{2,1,0:T(8,128)(2,1)} %broadcast_in_dim.15), calls=%async_computation.1 | async-start | bytes 2097152 | tf_op jit(solution)/shard_map/all_to_all | solution.py:198
  22.5 0.0 copy-start
  22.5 0.7 copy-done
  23.2 0.0 copy-start.3
  23.2 1.0 %copy-done.3 = f32[2,65536]{1,0:T(2,128)S(1)} copy-done((f32[2,65536]{1,0:T(2,128)S(1)}, f32[2,65536]{1,0:T(2,128)}, u32[]{:S(2)}) %copy-start.3) | copy-done | bytes 524312
  24.2 0.0 copy-start.4
  24.2 0.7 copy-done.4
  25.0 0.7 dense_tiles.1.dense_hbm
  25.7 9.7 %all-to-all-done.1 = bf16[4,32,4096]{2,1,0:T(8,128)(2,1)S(1)} async-done(((bf16[4,32,4096]{2,1,0:T(8,128)(2,1)}), bf16[4,32,4096]{2,1,0:T(8,128)(2,1)S(1)}, u32[]{:S(2)}, u32[]{:S(2)}) %all-to-all-start.1) | async-done | bytes 1048608 | tf_op jit(solution)/shard_map/all_to_all | solution.py:198
  35.4 0.0 copy-done.1
  35.4 0.0 copy-done.2
  35.4 3.6 %apply_row.3 = (f32[64,1024]{1,0:T(8,128)S(1)}, f32[64,1024]{1,0:T(8,128)S(1)}) custom-call(s32[2,16]{1,0:T(2,128)S(1)} %copy-done.1, s32[2,4]{1,0:T(2,128)S(1)} %copy-done.2, bf16[128,4096]{1,0:T(8,128)(2,1)S(1)} %bitcast.3, bf16[2,4,64,1024]{3,2,1,0:T(8,128)(2,1)} %bitcast.5, bf16[2,4,64,1024]{3,2,1,0:T(8,128)(2,1)} %bitcast.7, ...), custom_call_target="tpu_custom_call" | custom-call | flops 500000000 | bytes 8000000 | tf_op jit(solution)/shard_map/apply_row/pallas_call | solution.py:159
  39.0 3.6 %apply_row.2 = (f32[64,1024]{1,0:T(8,128)S(1)}, f32[64,1024]{1,0:T(8,128)S(1)}) custom-call(s32[2,16]{1,0:T(2,128)S(1)} %copy-done.1, s32[2,4]{1,0:T(2,128)S(1)} %copy-done.2, bf16[128,4096]{1,0:T(8,128)(2,1)S(1)} %bitcast.4, bf16[2,4,64,1024]{3,2,1,0:T(8,128)(2,1)} %bitcast.6, bf16[2,4,64,1024]{3,2,1,0:T(8,128)(2,1)} %bitcast.8, ...), custom_call_target="tpu_custom_call" | custom-call | flops 500000000 | bytes 8000000 | tf_op jit(solution)/shard_map/apply_row/pallas_call | solution.py:159
  42.7 1.9 %collective-permute-start.1 = (f32[64,1024]{1,0:T(8,128)S(1)}, f32[64,1024]{1,0:T(8,128)S(1)}, u32[]{:S(2)}, u32[]{:S(2)}) collective-permute-start(f32[64,1024]{1,0:T(8,128)S(1)} %get-tuple-element.12), channel_id=1, source_target_pairs={{0,1},{1,0},{2,3},{3,2},{4,5},{5,4},{6,7},{7,6},{8,9},{9,8},{10,11... | collective-permute-start | bytes 786440 | tf_op jit(solution)/shard_map/ppermute | solution.py:205
  44.6 2.4 %collective-permute-start = (f32[64,1024]{1,0:T(8,128)S(1)}, f32[64,1024]{1,0:T(8,128)S(1)}, u32[]{:S(2)}, u32[]{:S(2)}) collective-permute-start(f32[64,1024]{1,0:T(8,128)S(1)} %get-tuple-element.11), channel_id=1, source_target_pairs={{0,1},{1,0},{2,3},{3,2},{4,5},{5,4},{6,7},{7,6},{8,9},{9,8},{10,11... | collective-permute-start | bytes 786440 | tf_op jit(solution)/shard_map/ppermute | solution.py:205
  47.0 0.0 collective-permute-done.1.refs_3_
  47.0 1.1 %collective-permute-done.refs_2_ = f32[64,1024]{1,0:T(8,128)S(1)} collective-permute-done((f32[64,1024]{1,0:T(8,128)S(1)}, f32[64,1024]{1,0:T(8,128)S(1)}, u32[]{:S(2)}, u32[]{:S(2)}) %collective-permute-start) | collective-permute-done | bytes 262176 | tf_op jit(solution)/shard_map/ppermute | solution.py:205
  48.2 0.1 fold.1
  48.2 37.3 %all_to_all.16 = bf16[8,8,2048]{2,1,0:T(8,128)(2,1)S(1)} all-to-all(bf16[8,8,2048]{2,1,0:T(8,128)(2,1)S(1)} %fold.1), channel_id=1, replica_groups=mesh['y'=8,'x'=4,'z'=8,'c'=2] {'z'}, dimensions={0} | all-to-all | bytes 524288 | tf_op jit(solution)/shard_map/all_to_all | solution.py:212
  85.5 0.7 convert_reduce_fusion
Async XLA Ops:
  17.4 17.9 %copy-start.1 = (s32[2,16]{1,0:T(2,128)S(1)}, s32[2,16]{1,0:T(2,128)}, u32[]{:S(2)}) copy-start(s32[2,16]{1,0:T(2,128)} %near_ref.5) | copy-start | bytes 388
  17.5 17.9 %copy-start.2 = (s32[2,4]{1,0:T(2,128)S(1)}, s32[2,4]{1,0:T(2,128)}, u32[]{:S(2)}) copy-start(s32[2,4]{1,0:T(2,128)} %ranks_ref.3) | copy-start | bytes 100
  18.6 16.8 %all-to-all-start.1 = ((bf16[4,32,4096]{2,1,0:T(8,128)(2,1)}), bf16[4,32,4096]{2,1,0:T(8,128)(2,1)S(1)}, u32[]{:S(2)}, u32[]{:S(2)}) async-start(bf16[4,32,4096]{2,1,0:T(8,128)(2,1)} %broadcast_in_dim.15), calls=%async_computation.1 | async-start | bytes 2097152 | tf_op jit(solution)/shard_map/all_to_all | solution.py:198
  22.5 0.7 copy-start
  23.2 1.0 %copy-start.3 = (f32[2,65536]{1,0:T(2,128)S(1)}, f32[2,65536]{1,0:T(2,128)}, u32[]{:S(2)}) copy-start(f32[2,65536]{1,0:T(2,128)} %col_hbm.1) | copy-start | bytes 1572868
  24.2 0.7 copy-start.4
  42.7 4.3 %collective-permute-start.1 = (f32[64,1024]{1,0:T(8,128)S(1)}, f32[64,1024]{1,0:T(8,128)S(1)}, u32[]{:S(2)}, u32[]{:S(2)}) collective-permute-start(f32[64,1024]{1,0:T(8,128)S(1)} %get-tuple-element.12), channel_id=1, source_target_pairs={{0,1},{1,0},{2,3},{3,2},{4,5},{5,4},{6,7},{7,6},{8,9},{9,8},{10,11... | collective-permute-start | bytes 786440 | tf_op jit(solution)/shard_map/ppermute | solution.py:205
  44.6 3.6 %collective-permute-start = (f32[64,1024]{1,0:T(8,128)S(1)}, f32[64,1024]{1,0:T(8,128)S(1)}, u32[]{:S(2)}, u32[]{:S(2)}) collective-permute-start(f32[64,1024]{1,0:T(8,128)S(1)} %get-tuple-element.11), channel_id=1, source_target_pairs={{0,1},{1,0},{2,3},{3,2},{4,5},{5,4},{6,7},{7,6},{8,9},{9,8},{10,11... | collective-permute-start | bytes 786440 | tf_op jit(solution)/shard_map/ppermute | solution.py:205

commit v2 on v1

v2 whole, which is shorter than its diff:
```python
import functools

import jax
import jax.numpy as jnp
from jax import lax
from jax.experimental import pallas as pl
from jax.experimental.pallas import tpu as pltpu
from jax.sharding import Mesh, PartitionSpec as P

LOG2E = 1.4426950408889634
AXES = ("y", "x", "z", "c")
SIZES = (8, 4, 8, 2)
VMEM = pltpu.MemorySpace.VMEM
SMEM = pltpu.MemorySpace.SMEM
HBM = pltpu.MemorySpace.HBM


def first_column(cols_local):
    return (lax.axis_index("z") * 2 + lax.axis_index("c")) * cols_local


def is_near(near_ref, row, column):
    hit = near_ref[row, 0] == column
    for slot in range(1, near_ref.shape[1]):
        hit = jnp.logical_or(hit, near_ref[row, slot] == column)
    return hit


def dense_kernel(a, near_hbm, row_hbm, col_hbm, *refs):
    out_hbm, near_ref, line, coords, wide_x, wide_y, line_x, line_y, block, todo, sems, out_sems = refs[-12:]
    _, cols_local, tile, _ = out_hbm.shape
    first = first_column(cols_local)
    start = pl.multiple_of(first * tile, tile)
    fetches = [
        pltpu.make_async_copy(near_hbm, near_ref, sems.at[0]),
        pltpu.make_async_copy(row_hbm.at[:, pl.ds(a * tile, tile)], line, sems.at[1]),
        pltpu.make_async_copy(col_hbm.at[:, pl.ds(start, cols_local * tile)], coords, sems.at[2]),
    ]
    for fetch in fetches:
        fetch.start()
    fetches[0].wait()
    count = jnp.int32(0)
    for b in range(cols_local):
        todo[count] = b
        count = count + is_near(near_ref, a, first + b).astype(jnp.int32)
    fetches[1].wait()
    fetches[2].wait()
    line_x[...] = jnp.broadcast_to(line[0:1, :] * LOG2E, line_x.shape)
    line_y[...] = jnp.broadcast_to(line[1:2, :] * LOG2E, line_y.shape)
    step = 256

    def store(index):
        slot = lax.rem(index, 2)
        return pltpu.make_async_copy(block.at[slot], out_hbm.at[a, todo[index]], out_sems.at[slot])

    def make_tile(index, carry):
        b, slot = todo[index], lax.rem(index, 2)

        @pl.when(index >= 2)
        def _():
            store(index - 2).wait()

        for part in range(tile // 128):
            at = pl.multiple_of(b * tile + part * 128, 128)
            for axis, wide in ((0, wide_x), (1, wide_y)):
                piece = coords[axis : axis + 1, pl.ds(at, 128)] * LOG2E
                wide[part * 128 : (part + 1) * 128, :] = jnp.broadcast_to(piece, (128, 128)).T

        def body(k, carry):
            at = pl.multiple_of(k * step, step)
            for part in range(tile // 128):
                lanes = slice(part * 128, (part + 1) * 128)
                for q in range(0, step, 16):
                    rows = pl.ds(at + q, 16)
                    dx = wide_x[rows, :] - line_x[:, lanes]
                    dy = wide_y[rows, :] - line_y[:, lanes]
                    square = dx * dx + dy * dy
                    dist = square * lax.rsqrt(jnp.maximum(square, 1e-35))
                    block[slot, rows, lanes] = jnp.exp2(-dist).astype(jnp.bfloat16)
            return carry

        lax.fori_loop(0, tile // step, body, 0)
        store(index).start()
        return carry

    lax.fori_loop(0, count, make_tile, 0)
    for back in (2, 1):

        @pl.when(count >= back)
        def _(back=back):
            store(count - back).wait()


def dense_tiles(a, near, row_coords, col_coords, shape, made=None):
    _, cols_local, tile, _ = shape
    given = [near, row_coords, col_coords] + ([] if made is None else [made])
    return pl.pallas_call(
        functools.partial(dense_kernel, a),
        out_shape=HBM(shape, jnp.bfloat16),
        in_specs=[pl.BlockSpec(memory_space=HBM)] * len(given),
        out_specs=pl.BlockSpec(memory_space=HBM),
        input_output_aliases={} if made is None else {3: 0},
        scratch_shapes=[
            pltpu.SMEM(near.shape, jnp.int32),
            pltpu.VMEM((2, tile), jnp.float32),
            pltpu.VMEM((2, cols_local * tile), jnp.float32),
            pltpu.VMEM((tile, 128), jnp.float32),
            pltpu.VMEM((tile, 128), jnp.float32),
            pltpu.VMEM((16, tile), jnp.float32),
            pltpu.VMEM((16, tile), jnp.float32),
            pltpu.VMEM((2, tile, tile), jnp.bfloat16),
            pltpu.SMEM((cols_local + 1,), jnp.int32),
            pltpu.SemaphoreType.DMA((3,)),
            pltpu.SemaphoreType.DMA((2,)),
        ],
        compiler_params=pltpu.CompilerParams(vmem_limit_bytes=12 << 20),
        cost_estimate=pl.CostEstimate(flops=10_000_000, bytes_accessed=8_000_000, transcendentals=8_000_000),
        name="dense_tiles",
    )(*[pltpu.with_memory_space_constraint(g, HBM) for g in given])


def apply_kernel(near_ref, ranks_ref, draws_ref, v_ref, u_ref, dense_hbm, keep_ref, send_ref, total, dense, reduced, sems):
    rows_local, cols_local, rank, tile = v_ref.shape
    half = draws_ref.shape[0] // 2
    first = first_column(cols_local)
    tiles = [(a, b) for b in range(cols_local) for a in range(rows_local)]
    near = {(a, b): is_near(near_ref, a, first + b) for a, b in tiles}
    fetches = {
        (a, b): pltpu.make_async_copy(
            dense_hbm.at[a, b], dense.at[a * cols_local + b], sems.at[a * cols_local + b]
        )
        for a, b in tiles
    }
    for key in tiles:

        @pl.when(near[key])
        def _(key=key):
            fetches[key].start()

    for b in range(cols_local):
        lanes = slice(b * tile, (b + 1) * tile)
        both = jnp.concatenate([v_ref[a, b] for a in range(rows_local)], axis=0)
        sums = lax.dot_general(
            draws_ref[:, lanes], both, (((1,), (1,)), ((), ())), preferred_element_type=jnp.float32
        )
        ids = lax.broadcasted_iota(jnp.int32, sums.shape, 1)
        limit = jnp.int32(0)
        for a in reversed(range(rows_local)):
            end = a * rank + jnp.where(near[a, b], 0, ranks_ref[a, b])
            limit = jnp.where(ids < (a + 1) * rank, end, limit)
        sums = jnp.where(ids < limit, sums, 0.0).astype(jnp.bfloat16)
        for a in range(rows_local):
            reduced[a, :, b * rank : (b + 1) * rank] = sums[:, a * rank : (a + 1) * rank]
    for a in range(rows_local):
        for at in range(0, tile, 256):
            part = slice(at, at + 256)
            left = u_ref[a, :, :, part].reshape(cols_local * rank, 256)
            total[:, a * tile + at : a * tile + at + 256] = jnp.dot(
                reduced[a], left, preferred_element_type=jnp.float32
            )
    for a, b in tiles:

        @pl.when(near[a, b])
        def _(a=a, b=b):
            fetches[a, b].wait()
            piece = draws_ref[:, b * tile : (b + 1) * tile]
            for at in range(0, tile, 256):
                product = jnp.dot(
                    piece, dense[a * cols_local + b, :, at : at + 256], preferred_element_type=jnp.float32
                )
                total[:, a * tile + at : a * tile + at + 256] += product * 0.03125

    core = lax.axis_index("c")
    keep_ref[...] = total[pl.ds(pl.multiple_of(core * half, half), half), :]
    send_ref[...] = total[pl.ds(pl.multiple_of((1 - core) * half, half), half), :]


def apply_tiles(near, ranks, draws, v_factors, u_factors, dense):
    rows_local, cols_local, rank, tile = v_factors.shape
    width = draws.shape[0]
    half = jax.ShapeDtypeStruct((width // 2, rows_local * tile), jnp.float32)
    count = rows_local * cols_local
    return pl.pallas_call(
        apply_kernel,
        out_shape=(half, half),
        in_specs=[pl.BlockSpec(memory_space=SMEM)] * 2
        + [pl.BlockSpec(memory_space=VMEM)] * 3
        + [pl.BlockSpec(memory_space=HBM)],
        out_specs=(pl.BlockSpec(memory_space=VMEM),) * 2,
        scratch_shapes=[
            pltpu.VMEM((width, rows_local * tile), jnp.float32),
            pltpu.VMEM((count, tile, tile), jnp.bfloat16),
            pltpu.VMEM((rows_local, width, cols_local * rank), jnp.bfloat16),
            pltpu.SemaphoreType.DMA((count,)),
        ],
        compiler_params=pltpu.CompilerParams(vmem_limit_bytes=32 << 20),
        cost_estimate=pl.CostEstimate(flops=1_000_000_000, bytes_accessed=16_000_000, transcendentals=0),
        name="apply_tiles",
    )(near, ranks, draws, v_factors, u_factors, pltpu.with_memory_space_constraint(dense, HBM))


def fold_kernel(keep_ref, other_ref, out_ref):
    both = keep_ref[...] + other_ref[...]
    for z in range(out_ref.shape[0]):
        block = jnp.concatenate([both[4 * z : 4 * z + 4], both[32 + 4 * z : 36 + 4 * z]], axis=0)
        out_ref[z] = block.astype(jnp.bfloat16)


def per_device(draws, u_factors, v_factors, ranks, near, row_coords, col_coords):
    rows_local, cols_local, tile, rank = u_factors.shape
    ny, nx, nz, nc = SIZES
    own = draws.shape[0]
    span = draws.shape[1]
    u_t = jnp.swapaxes(u_factors, 2, 3)
    v_t = jnp.swapaxes(v_factors, 2, 3)
    shape = (rows_local, cols_local, tile, tile)
    column = lax.all_to_all(jnp.broadcast_to(draws[None], (ny, own, span)), "y", 0, 0)
    dense = dense_tiles(0, near, row_coords, col_coords, shape)
    column, dense, late = lax.optimization_barrier((column, dense, near))
    column = column.reshape(ny * own, span)
    plane = lax.all_to_all(jnp.broadcast_to(column[None], (nx, ny * own, span)), "x", 0, 0)
    dense = dense_tiles(1, late, row_coords, col_coords, shape, dense)
    plane = plane.reshape(nx * ny * own, span)
    keep, send = apply_tiles(near, ranks, plane, v_t, u_t, dense)
    pairs = [(i, i ^ 1) for i in range(nz * nc)]
    other = lax.ppermute(send, ("z", "c"), pairs)
    blocks = pl.pallas_call(
        fold_kernel,
        out_shape=jax.ShapeDtypeStruct((nz, 8, rows_local * tile), jnp.bfloat16),
        compiler_params=pltpu.CompilerParams(vmem_limit_bytes=6 << 20),
        name="fold",
    )(keep, other)
    spread = lax.all_to_all(blocks, "z", 0, 0)
    return jnp.sum(spread.astype(jnp.float32), axis=0)


def solution(mesh):
    fine = Mesh(mesh.devices.reshape(SIZES), AXES)
    row, col = ("y", "x"), ("z", "c")
    return jax.shard_map(
        per_device,
        mesh=fine,
        in_specs=(
            P(row, col),
            P(row, col, None, None),
            P(row, col, None, None),
            P(row, col),
            P(row, None),
            P(None, row),
            P(),
        ),
        out_specs=P(col, row),
        check_vma=False,
    )
```

time: 86.9 us -> 70.8 us (0.81)
  blocking collectives: 53.8 us -> 27 us
  waiting for transfers between devices: 10.8 us -> 21.9 us
  starting transfers between devices: 8.29 us -> 14.6 us
  Pallas kernels: 8.1 us -> 3.4 us
  local copies, waits for them, and re-layouts: 4.42 us -> 2.68 us
    all_to_all x1 -> x0, blocking collectives: 16.5 us -> none  [per_device(): lax.all_to_all(jnp.broadcast_to(draws[None], (ny, own, span)), 'y', 0, 0)]
    all_to_all x1, blocking collectives: 37.3 us -> 27 us  [per_device(): spread = lax.all_to_all(blocks, 'z', 0, 0)]
    all_to_all x0 -> x1, starting transfers between devices: none -> 9.03 us  [per_device(): lax.all_to_all(jnp.broadcast_to(draws[None], (ny, own, span)), 'y', 0, 0)]
    all_to_all x0 -> x1, waiting for transfers between devices: none -> 7.16 us  [per_device(): lax.all_to_all(jnp.broadcast_to(draws[None], (ny, own, span)), 'y', 0, 0)]
    pallas_call x3, Pallas kernels: 8.02 us -> 3.31 us  [the longest x2 1.82 us: dense_tiles(): pl.pallas_call(functools.partial(dense_kernel, a), out_shape=HBM(shape, j...]
    all_to_all x1, waiting for transfers between devices: 9.67 us -> 12.8 us  [per_device(): lax.all_to_all(jnp.broadcast_to(column[None], (nx, ny * own, span)), 'x',...]
    unnamed x10 -> x8, local copies, waits for them, and re-layouts: 2.45 us -> 0.02 us
    ppermute x2 -> x1, starting transfers between devices: 4.33 us -> 1.92 us  [per_device(): other = lax.ppermute(send, ('z', 'c'), pairs)]
  transfers between devices with their start and end apart: 3 -> 3, of which waited for: 2 -> 3; matrix products, arithmetic and copies ran while one was open for 0% -> 0% of each run, Pallas kernels for 1% -> 3%
where the time goes in v2:
time: 70.8 us; the launch traced here: 70.3 us
  blocking collectives  27 us (38%)
  waiting for transfers between devices  21.9 us (31%)
  starting transfers between devices  14.6 us (21%)
  Pallas kernels  3.4 us (5%)
  local copies, waits for them, and re-layouts  2.68 us (4%)
    all_to_all x1, blocking collectives, per_device(): spread = lax.all_to_all(blocks, 'z', 0, 0)  27 us
    all_to_all x1, waiting for transfers between devices, per_device(): lax.all_to_all(jnp.broadcast_to(column[None], (nx, ny * own, span)), 'x',...  12.8 us
    all_to_all x1, starting transfers between devices, per_device(): lax.all_to_all(jnp.broadcast_to(draws[None], (ny, own, span)), 'y', 0, 0)  9.03 us
    all_to_all x1, waiting for transfers between devices, per_device(): lax.all_to_all(jnp.broadcast_to(draws[None], (ny, own, span)), 'y', 0, 0)  7.16 us
    all_to_all x1, starting transfers between devices, per_device(): lax.all_to_all(jnp.broadcast_to(column[None], (nx, ny * own, span)), 'x',...  3.68 us
    ppermute x1, starting transfers between devices, per_device(): other = lax.ppermute(send, ('z', 'c'), pairs)  1.92 us
    ppermute x1, waiting for transfers between devices, per_device(): other = lax.ppermute(send, ('z', 'c'), pairs)  1.88 us
    pallas_call x2, Pallas kernels, dense_tiles(): pl.pallas_call(functools.partial(dense_kernel, a), out_shape=HBM(shape, j...  1.82 us
  transfers between devices with their start and end apart: 3, of which 3 were waited for; matrix products, arithmetic and copies ran while one was open for 0% of the time, Pallas kernels for 3%

profile of v2, /device:TPU:16, one launch (start us, length us, event | category | flops | bytes accessed | tf_op | source)
XLA Modules:
  0.0 70.3 jit_solution(15484511938744482096)
XLA Ops:
  0.0 1.5 %broadcast_in_dim.6 = bf16[8,4,4096]{2,1,0:T(4,128)(2,1)} broadcast(bf16[4,4096]{1,0:T(4,128)(2,1)} %param.7), dimensions={1,2} | broadcast | bytes 294912 | tf_op jit(solution)/shard_map/broadcast_in_dim | solution.py:217
  1.5 9.0 %all-to-all-start = ((bf16[8,4,4096]{2,1,0:T(4,128)(2,1)}), bf16[8,4,4096]{2,1,0:T(4,128)(2,1)S(1)}, u32[]{:S(2)}, u32[]{:S(2)}) async-start(bf16[8,4,4096]{2,1,0:T(4,128)(2,1)} %broadcast_in_dim.6), calls=%async_computation | async-start | bytes 524288 | tf_op jit(solution)/shard_map/all_to_all | solution.py:217
  10.6 0.8 %dense_tiles.2.refs_0_ = bf16[2,4,1024,1024]{3,2,1,0:T(8,128)(2,1)} custom-call(s32[2,16]{1,0:T(2,128)} %near_ref.1, f32[2,2048]{1,0:T(2,128)} %row_hbm.3, f32[2,65536]{1,0:T(2,128)} %col_hbm.3), custom_call_target="tpu_custom_call" | custom-call | flops 10000000 | bytes 8000000 | tf_op jit(solution)/shard_map/dense_tiles/pallas_call | solution.py:97
  11.4 7.2 %all-to-all-done = bf16[8,4,4096]{2,1,0:T(4,128)(2,1)S(1)} async-done(((bf16[8,4,4096]{2,1,0:T(4,128)(2,1)}), bf16[8,4,4096]{2,1,0:T(4,128)(2,1)S(1)}, u32[]{:S(2)}, u32[]{:S(2)}) %all-to-all-start) | async-done | bytes 262176 | tf_op jit(solution)/shard_map/all_to_all | solution.py:217
  18.6 0.1 broadcast_in_dim.14
  18.6 1.1 %broadcast_in_dim.15 = bf16[4,32,4096]{2,1,0:T(8,128)(2,1)} broadcast(bf16[32,4096]{1,0:T(8,128)(2,1)S(1)} %broadcast_in_dim.14), dimensions={1,2} | broadcast | bytes 1310720 | tf_op jit(solution)/shard_map/broadcast_in_dim | solution.py:221
  19.7 3.7 %all-to-all-start.1 = ((bf16[4,32,4096]{2,1,0:T(8,128)(2,1)}), bf16[4,32,4096]{2,1,0:T(8,128)(2,1)S(1)}, u32[]{:S(2)}, u32[]{:S(2)}) async-start(bf16[4,32,4096]{2,1,0:T(8,128)(2,1)} %broadcast_in_dim.15), calls=%async_computation.1 | async-start | bytes 2097152 | tf_op jit(solution)/shard_map/all_to_all | solution.py:221
  23.4 0.0 copy-start
  23.4 0.0 copy-start.1
  23.4 0.0 copy-start.2
  23.4 0.0 copy-start.3
  23.4 1.0 %dense_tiles.3.dense_hbm = bf16[2,4,1024,1024]{3,2,1,0:T(8,128)(2,1)} custom-call(s32[2,16]{1,0:T(2,128)} %near_ref.1, f32[2,2048]{1,0:T(2,128)} %row_hbm.3, f32[2,65536]{1,0:T(2,128)} %col_hbm.3, bf16[2,4,1024,1024]{3,2,1,0:T(8,128)(2,1)} %dense_tiles.2.refs_0_), custom_call_target="tpu_custom_call", output_to_operand_aliasing={{}: (3, {})} | custom-call | flops 10000000 | bytes 8000000 | tf_op jit(solution)/shard_map/dense_tiles/pallas_call | solution.py:97
  24.4 12.8 %all-to-all-done.1 = bf16[4,32,4096]{2,1,0:T(8,128)(2,1)S(1)} async-done(((bf16[4,32,4096]{2,1,0:T(8,128)(2,1)}), bf16[4,32,4096]{2,1,0:T(8,128)(2,1)S(1)}, u32[]{:S(2)}, u32[]{:S(2)}) %all-to-all-start.1) | async-done | bytes 1048608 | tf_op jit(solution)/shard_map/all_to_all | solution.py:221
  37.2 0.0 copy-done
  37.2 0.0 copy-done.1
  37.2 0.0 copy-done.2
  37.2 0.0 copy-done.3
  37.3 1.5 %apply_tiles.1 = (f32[64,2048]{1,0:T(8,128)S(1)}, f32[64,2048]{1,0:T(8,128)S(1)}) custom-call(s32[2,16]{1,0:T(2,128)S(1)} %copy-done.2, s32[2,4]{1,0:T(2,128)S(1)} %copy-done.3, bf16[128,4096]{1,0:T(8,128)(2,1)S(1)} %bitcast.3, bf16[2,4,64,1024]{3,2,1,0:T(8,128)(2,1)S(1)} %bitcast.4, bf16[2,4,64,1024]{3,2,1,0:T(8,128)(2,1)S(1)} %bitcast.5, ...), custom_call_target="tpu_custom_call" | custom-call | flops 1000000000 | bytes 16000000 | tf_op jit(solution)/shard_map/apply_tiles/pallas_call | solution.py:183
  38.8 1.9 %collective-permute-start = (f32[64,2048]{1,0:T(8,128)S(1)}, f32[64,2048]{1,0:T(8,128)S(1)}, u32[]{:S(2)}, u32[]{:S(2)}) collective-permute-start(f32[64,2048]{1,0:T(8,128)S(1)} %get-tuple-element.14), channel_id=1, source_target_pairs={{0,1},{1,0},{2,3},{3,2},{4,5},{5,4},{6,7},{7,6},{8,9},{9,8},{10,11... | collective-permute-start | bytes 1572872 | tf_op jit(solution)/shard_map/ppermute | solution.py:226
  40.7 1.9 %collective-permute-done.other_ref = f32[64,2048]{1,0:T(8,128)S(1)} collective-permute-done((f32[64,2048]{1,0:T(8,128)S(1)}, f32[64,2048]{1,0:T(8,128)S(1)}, u32[]{:S(2)}, u32[]{:S(2)}) %collective-permute-start) | collective-permute-done | bytes 524320 | tf_op jit(solution)/shard_map/ppermute | solution.py:226
  42.6 0.1 fold.1
  42.7 27.0 %all_to_all.15 = bf16[8,8,2048]{2,1,0:T(8,128)(2,1)S(1)} all-to-all(bf16[8,8,2048]{2,1,0:T(8,128)(2,1)S(1)} %fold.1), channel_id=1, replica_groups=mesh['y'=8,'x'=4,'z'=8,'c'=2] {'z'}, dimensions={0} | all-to-all | bytes 524288 | tf_op jit(solution)/shard_map/all_to_all | solution.py:233
  69.7 0.7 convert_reduce_fusion
Async XLA Ops:
  1.5 17.0 %all-to-all-start = ((bf16[8,4,4096]{2,1,0:T(4,128)(2,1)}), bf16[8,4,4096]{2,1,0:T(4,128)(2,1)S(1)}, u32[]{:S(2)}, u32[]{:S(2)}) async-start(bf16[8,4,4096]{2,1,0:T(4,128)(2,1)} %broadcast_in_dim.6), calls=%async_computation | async-start | bytes 524288 | tf_op jit(solution)/shard_map/all_to_all | solution.py:217
  19.7 17.5 %all-to-all-start.1 = ((bf16[4,32,4096]{2,1,0:T(8,128)(2,1)}), bf16[4,32,4096]{2,1,0:T(8,128)(2,1)S(1)}, u32[]{:S(2)}, u32[]{:S(2)}) async-start(bf16[4,32,4096]{2,1,0:T(8,128)(2,1)} %broadcast_in_dim.15), calls=%async_computation.1 | async-start | bytes 2097152 | tf_op jit(solution)/shard_map/all_to_all | solution.py:221
  23.4 13.8 %copy-start = (bf16[2,4,1024,64]{2,3,1,0:T(8,128)(2,1)S(1)}, bf16[2,4,1024,64]{2,3,1,0:T(8,128)(2,1)}, u32[]{:S(2)}) copy-start(bf16[2,4,1024,64]{2,3,1,0:T(8,128)(2,1)} %param.9) | copy-start | bytes 3145732
  23.4 13.8 %copy-start.1 = (bf16[2,4,1024,64]{2,3,1,0:T(8,128)(2,1)S(1)}, bf16[2,4,1024,64]{2,3,1,0:T(8,128)(2,1)}, u32[]{:S(2)}) copy-start(bf16[2,4,1024,64]{2,3,1,0:T(8,128)(2,1)} %param.8) | copy-start | bytes 3145732
  23.4 13.8 %copy-start.2 = (s32[2,16]{1,0:T(2,128)S(1)}, s32[2,16]{1,0:T(2,128)}, u32[]{:S(2)}) copy-start(s32[2,16]{1,0:T(2,128)} %near_ref.1) | copy-start | bytes 388
  23.4 13.8 %copy-start.3 = (s32[2,4]{1,0:T(2,128)S(1)}, s32[2,4]{1,0:T(2,128)}, u32[]{:S(2)}) copy-start(s32[2,4]{1,0:T(2,128)} %ranks_ref.1) | copy-start | bytes 100
  38.8 3.8 %collective-permute-start = (f32[64,2048]{1,0:T(8,128)S(1)}, f32[64,2048]{1,0:T(8,128)S(1)}, u32[]{:S(2)}, u32[]{:S(2)}) collective-permute-start(f32[64,2048]{1,0:T(8,128)S(1)} %get-tuple-element.14), channel_id=1, source_target_pairs={{0,1},{1,0},{2,3},{3,2},{4,5},{5,4},{6,7},{7,6},{8,9},{9,8},{10,11... | collective-permute-start | bytes 1572872 | tf_op jit(solution)/shard_map/ppermute | solution.py:226

commit v3 on v2

--- a/solution.py
+++ b/solution.py
@@ -2,6 +2,7 @@
 
 import jax
 import jax.numpy as jnp
+import numpy as np
 from jax import lax
 from jax.experimental import pallas as pl
 from jax.experimental.pallas import tpu as pltpu
@@ -15,6 +16,25 @@
 HBM = pltpu.MemorySpace.HBM
 
 
+Y_ORDER = (0, 4, 2, 6, 1, 5, 3, 7)
+Z_ORDER = (0, 3, 6, 1, 4, 7, 2, 5)
+X_ORDER = (0, 1, 2, 3)
+
+
+def orders(order):
+    return order, order[::-1]
+
+
+def partners(axis, order):
+    ids = np.arange(np.prod(SIZES)).reshape(SIZES)
+    lines = np.moveaxis(ids, AXES.index(axis), -1)
+    groups = []
+    for core, places in enumerate(orders(order)):
+        one = lines[..., core, :] if axis != "c" else lines
+        groups += one[..., list(places)].reshape(-1, len(order)).tolist()
+    return groups
+
+
 def first_column(cols_local):
     return (lax.axis_index("z") * 2 + lax.axis_index("c")) * cols_local
 
@@ -26,14 +46,14 @@
     return hit
 
 
-def dense_kernel(a, near_hbm, row_hbm, col_hbm, *refs):
-    out_hbm, near_ref, line, coords, wide_x, wide_y, line_x, line_y, block, todo, sems, out_sems = refs[-12:]
-    _, cols_local, tile, _ = out_hbm.shape
+def dense_kernel(low, high, near_hbm, row_hbm, col_hbm, *refs):
+    out_hbm, near_ref, lines, coords, wide_x, wide_y, line_x, line_y, block, todo, sems, out_sems = refs[-12:]
+    rows_local, cols_local, tile, _ = out_hbm.shape
     first = first_column(cols_local)
     start = pl.multiple_of(first * tile, tile)
     fetches = [
         pltpu.make_async_copy(near_hbm, near_ref, sems.at[0]),
-        pltpu.make_async_copy(row_hbm.at[:, pl.ds(a * tile, tile)], line, sems.at[1]),
+        pltpu.make_async_copy(row_hbm, lines, sems.at[1]),
         pltpu.make_async_copy(col_hbm.at[:, pl.ds(start, cols_local * tile)], coords, sems.at[2]),
     ]
     for fetch in fetches:
@@ -41,30 +61,43 @@
     fetches[0].wait()
     count = jnp.int32(0)
     for b in range(cols_local):
-        todo[count] = b
-        count = count + is_near(near_ref, a, first + b).astype(jnp.int32)
+        for a in range(rows_local):
+            todo[count] = b * rows_local + a
+            count = count + is_near(near_ref, a, first + b).astype(jnp.int32)
     fetches[1].wait()
     fetches[2].wait()
-    line_x[...] = jnp.broadcast_to(line[0:1, :] * LOG2E, line_x.shape)
-    line_y[...] = jnp.broadcast_to(line[1:2, :] * LOG2E, line_y.shape)
+    begin, end = jnp.minimum(count, low), jnp.minimum(count, high)
     step = 256
 
-    def store(index):
-        slot = lax.rem(index, 2)
-        return pltpu.make_async_copy(block.at[slot], out_hbm.at[a, todo[index]], out_sems.at[slot])
+    @pl.when(begin < end)
+    def _():
+        for a in range(rows_local):
+            lanes = slice(a * tile, (a + 1) * tile)
+            line_x[a] = jnp.broadcast_to(lines[0:1, lanes] * LOG2E, line_x.shape[1:])
+            line_y[a] = jnp.broadcast_to(lines[1:2, lanes] * LOG2E, line_y.shape[1:])
+
+    def place(index):
+        return lax.rem(todo[index], rows_local), lax.div(todo[index], rows_local), lax.rem(index, 2)
+
+    def store(index, at=0, size=tile):
+        a, b, slot = place(index)
+        rows = pl.ds(at, size)
+        return pltpu.make_async_copy(block.at[slot, rows], out_hbm.at[a, b, rows], out_sems.at[slot])
 
     def make_tile(index, carry):
-        b, slot = todo[index], lax.rem(index, 2)
-
-        @pl.when(index >= 2)
+        a, b, slot = place(index)
+
+        @pl.when(index >= begin + 2)
         def _():
             store(index - 2).wait()
 
-        for part in range(tile // 128):
-            at = pl.multiple_of(b * tile + part * 128, 128)
-            for axis, wide in ((0, wide_x), (1, wide_y)):
-                piece = coords[axis : axis + 1, pl.ds(at, 128)] * LOG2E
-                wide[part * 128 : (part + 1) * 128, :] = jnp.broadcast_to(piece, (128, 128)).T
+        @pl.when(jnp.logical_or(index == begin, b != place(jnp.maximum(index - 1, 0))[1]))
+        def _():
+            for part in range(tile // 128):
+                at = pl.multiple_of(b * tile + part * 128, 128)
+                for axis, wide in ((0, wide_x), (1, wide_y)):
+                    piece = coords[axis : axis + 1, pl.ds(at, 128)] * LOG2E
+                    wide[part * 128 : (part + 1) * 128, :] = jnp.broadcast_to(piece, (128, 128)).T
 
         def body(k, carry):
             at = pl.multiple_of(k * step, step)
@@ -72,44 +105,44 @@
                 lanes = slice(part * 128, (part + 1) * 128)
                 for q in range(0, step, 16):
                     rows = pl.ds(at + q, 16)
-                    dx = wide_x[rows, :] - line_x[:, lanes]
-                    dy = wide_y[rows, :] - line_y[:, lanes]
+                    dx = wide_x[rows, :] - line_x[a, :, lanes]
+                    dy = wide_y[rows, :] - line_y[a, :, lanes]
                     square = dx * dx + dy * dy
                     dist = square * lax.rsqrt(jnp.maximum(square, 1e-35))
                     block[slot, rows, lanes] = jnp.exp2(-dist).astype(jnp.bfloat16)
+            store(index, at, step).start()
             return carry
 
         lax.fori_loop(0, tile // step, body, 0)
-        store(index).start()
         return carry
 
-    lax.fori_loop(0, count, make_tile, 0)
+    lax.fori_loop(begin, end, make_tile, 0)
     for back in (2, 1):
 
-        @pl.when(count >= back)
+        @pl.when(end - begin >= back)
         def _(back=back):
-            store(count - back).wait()
-
-
-def dense_tiles(a, near, row_coords, col_coords, shape, made=None):
-    _, cols_local, tile, _ = shape
+            store(end - back).wait()
+
+
+def dense_tiles(low, high, near, row_coords, col_coords, shape, made=None):
+    rows_local, cols_local, tile, _ = shape
     given = [near, row_coords, col_coords] + ([] if made is None else [made])
     return pl.pallas_call(
-        functools.partial(dense_kernel, a),
+        functools.partial(dense_kernel, low, high),
         out_shape=HBM(shape, jnp.bfloat16),
         in_specs=[pl.BlockSpec(memory_space=HBM)] * len(given),
         out_specs=pl.BlockSpec(memory_space=HBM),
         input_output_aliases={} if made is None else {3: 0},
         scratch_shapes=[
             pltpu.SMEM(near.shape, jnp.int32),
-            pltpu.VMEM((2, tile), jnp.float32),
+            pltpu.VMEM(row_coords.shape, jnp.float32),
             pltpu.VMEM((2, cols_local * tile), jnp.float32),
             pltpu.VMEM((tile, 128), jnp.float32),
             pltpu.VMEM((tile, 128), jnp.float32),
-            pltpu.VMEM((16, tile), jnp.float32),
-            pltpu.VMEM((16, tile), jnp.float32),
+            pltpu.VMEM((rows_local, 16, tile), jnp.float32),
+            pltpu.VMEM((rows_local, 16, tile), jnp.float32),
             pltpu.VMEM((2, tile, tile), jnp.bfloat16),
-            pltpu.SMEM((cols_local + 1,), jnp.int32),
+            pltpu.SMEM((rows_local * cols_local + 1,), jnp.int32),
             pltpu.SemaphoreType.DMA((3,)),
             pltpu.SemaphoreType.DMA((2,)),
         ],
@@ -124,7 +157,7 @@
     half = draws_ref.shape[0] // 2
     first = first_column(cols_local)
     tiles = [(a, b) for b in range(cols_local) for a in range(rows_local)]
-    near = {(a, b): is_near(near_ref, a, first + b) for a, b in tiles}
+    near = {}
     fetches = {
         (a, b): pltpu.make_async_copy(
             dense_hbm.at[a, b], dense.at[a * cols_local + b], sems.at[a * cols_local + b]
@@ -132,6 +165,7 @@
         for a, b in tiles
     }
     for key in tiles:
+        near[key] = is_near(near_ref, key[0], first + key[1])
 
         @pl.when(near[key])
         def _(key=key):
@@ -170,9 +204,8 @@
                 )
                 total[:, a * tile + at : a * tile + at + 256] += product * 0.03125
 
-    core = lax.axis_index("c")
-    keep_ref[...] = total[pl.ds(pl.multiple_of(core * half, half), half), :]
-    send_ref[...] = total[pl.ds(pl.multiple_of((1 - core) * half, half), half), :]
+    keep_ref[...] = total[:half, :]
+    send_ref[...] = total[half:, :]
 
 
 def apply_tiles(near, ranks, draws, v_factors, u_factors, dense):
@@ -200,10 +233,17 @@
 
 
 def fold_kernel(keep_ref, other_ref, out_ref):
-    both = keep_ref[...] + other_ref[...]
-    for z in range(out_ref.shape[0]):
-        block = jnp.concatenate([both[4 * z : 4 * z + 4], both[32 + 4 * z : 36 + 4 * z]], axis=0)
-        out_ref[z] = block.astype(jnp.bfloat16)
+    blocks = out_ref.shape[0]
+    core = lax.axis_index("c")
+    for at in range(blocks):
+        back = blocks - 1 - at
+        first = keep_ref[4 * at : 4 * at + 4] + other_ref[32 + 4 * back : 36 + 4 * back]
+        second = keep_ref[32 + 4 * at : 36 + 4 * at] + other_ref[4 * back : 4 * back + 4]
+        lower = jnp.where(core == 0, first, second)
+        upper = jnp.where(core == 0, second, first)
+        places = [z.index(y[at]) for y, z in zip(orders(Y_ORDER), orders(Z_ORDER))]
+        place = jnp.where(core == 0, places[0], places[1])
+        out_ref[place] = jnp.concatenate([lower, upper], axis=0).astype(jnp.bfloat16)
 
 
 def per_device(draws, u_factors, v_factors, ranks, near, row_coords, col_coords):
@@ -214,12 +254,14 @@
     u_t = jnp.swapaxes(u_factors, 2, 3)
     v_t = jnp.swapaxes(v_factors, 2, 3)
     shape = (rows_local, cols_local, tile, tile)
-    column = lax.all_to_all(jnp.broadcast_to(draws[None], (ny, own, span)), "y", 0, 0)
-    dense = dense_tiles(0, near, row_coords, col_coords, shape)
+    copies = jnp.broadcast_to(draws[None], (ny, own, span))
+    column = lax.all_to_all(copies, AXES, 0, 0, axis_index_groups=partners("y", Y_ORDER))
+    dense = dense_tiles(0, 3, near, row_coords, col_coords, shape)
     column, dense, late = lax.optimization_barrier((column, dense, near))
     column = column.reshape(ny * own, span)
-    plane = lax.all_to_all(jnp.broadcast_to(column[None], (nx, ny * own, span)), "x", 0, 0)
-    dense = dense_tiles(1, late, row_coords, col_coords, shape, dense)
+    copies = jnp.broadcast_to(column[None], (nx, ny * own, span))
+    plane = lax.all_to_all(copies, AXES, 0, 0, axis_index_groups=partners("x", X_ORDER))
+    dense = dense_tiles(3, 8, late, row_coords, col_coords, shape, dense)
     plane = plane.reshape(nx * ny * own, span)
     keep, send = apply_tiles(near, ranks, plane, v_t, u_t, dense)
     pairs = [(i, i ^ 1) for i in range(nz * nc)]
@@ -230,7 +272,7 @@
         compiler_params=pltpu.CompilerParams(vmem_limit_bytes=6 << 20),
         name="fold",
     )(keep, other)
-    spread = lax.all_to_all(blocks, "z", 0, 0)
+    spread = lax.all_to_all(blocks, AXES, 0, 0, axis_index_groups=partners("z", Z_ORDER))
     return jnp.sum(spread.astype(jnp.float32), axis=0)
 
 

time: 70.8 us -> 68.6 us (0.969)
  the two profiles are of different devices: /device:TPU:16 before, /device:TPU:30 now
where the time goes in v3:
time: 68.6 us; the launch traced here: 68.2 us
  blocking collectives  27.5 us (40%)
  waiting for transfers between devices  19 us (28%)
  starting transfers between devices  14.8 us (22%)
  Pallas kernels  3.5 us (5%)
  local copies, waits for them, and re-layouts  2.68 us (4%)
    all_to_all x1, blocking collectives, per_device(): lax.all_to_all(blocks, AXES, 0, 0, axis_index_groups=partners('z', Z_ORDER))  27.5 us
    all_to_all x1, waiting for transfers between devices, per_device(): lax.all_to_all(copies, AXES, 0, 0, axis_index_groups=partners('x', X_ORDER))  11.1 us
    all_to_all x1, starting transfers between devices, per_device(): lax.all_to_all(copies, AXES, 0, 0, axis_index_groups=partners('y', Y_ORDER))  7.32 us
    all_to_all x1, waiting for transfers between devices, per_device(): lax.all_to_all(copies, AXES, 0, 0, axis_index_groups=partners('y', Y_ORDER))  6.01 us
    all_to_all x1, starting transfers between devices, per_device(): lax.all_to_all(copies, AXES, 0, 0, axis_index_groups=partners('x', X_ORDER))  5.55 us
    ppermute x1, starting transfers between devices, per_device(): other = lax.ppermute(send, ('z', 'c'), pairs)  1.92 us
    ppermute x1, waiting for transfers between devices, per_device(): other = lax.ppermute(send, ('z', 'c'), pairs)  1.88 us
    pallas_call x2, Pallas kernels, dense_tiles(): pl.pallas_call(functools.partial(dense_kernel, low, high), out_shape=HBM(...  1.86 us
  transfers between devices with their start and end apart: 3, of which 3 were waited for; matrix products, arithmetic and copies ran while one was open for 0% of the time, Pallas kernels for 3%

profile of v3, /device:TPU:30, one launch (start us, length us, event | category | flops | bytes accessed | tf_op | source)
XLA Modules:
  0.0 68.2 jit_solution(9024570978096263992)
XLA Ops:
  0.0 1.5 %broadcast_in_dim.6 = bf16[8,4,4096]{2,1,0:T(4,128)(2,1)} broadcast(bf16[4,4096]{1,0:T(4,128)(2,1)} %param.7), dimensions={1,2} | broadcast | bytes 294912 | tf_op jit(solution)/shard_map/broadcast_in_dim | solution.py:257
  1.5 7.3 %all-to-all-start = ((bf16[8,4,4096]{2,1,0:T(4,128)(2,1)}), bf16[8,4,4096]{2,1,0:T(4,128)(2,1)S(1)}, u32[]{:S(2)}, u32[]{:S(2)}) async-start(bf16[8,4,4096]{2,1,0:T(4,128)(2,1)} %broadcast_in_dim.6), calls=%async_computation | async-start | bytes 524288 | tf_op jit(solution)/shard_map/all_to_all | solution.py:258
  8.9 0.9 %dense_tiles.2.refs_0_ = bf16[2,4,1024,1024]{3,2,1,0:T(8,128)(2,1)} custom-call(s32[2,16]{1,0:T(2,128)} %near_ref.1, f32[2,2048]{1,0:T(2,128)} %row_hbm.3, f32[2,65536]{1,0:T(2,128)} %col_hbm.3), custom_call_target="tpu_custom_call" | custom-call | flops 10000000 | bytes 8000000 | tf_op jit(solution)/shard_map/dense_tiles/pallas_call | solution.py:130
  9.7 6.0 %all-to-all-done = bf16[8,4,4096]{2,1,0:T(4,128)(2,1)S(1)} async-done(((bf16[8,4,4096]{2,1,0:T(4,128)(2,1)}), bf16[8,4,4096]{2,1,0:T(4,128)(2,1)S(1)}, u32[]{:S(2)}, u32[]{:S(2)}) %all-to-all-start) | async-done | bytes 262176 | tf_op jit(solution)/shard_map/all_to_all | solution.py:258
  15.7 0.1 broadcast_in_dim.14
  15.8 1.1 %broadcast_in_dim.15 = bf16[4,32,4096]{2,1,0:T(8,128)(2,1)} broadcast(bf16[32,4096]{1,0:T(8,128)(2,1)S(1)} %broadcast_in_dim.14), dimensions={1,2} | broadcast | bytes 1310720 | tf_op jit(solution)/shard_map/broadcast_in_dim | solution.py:262
  16.9 5.5 %all-to-all-start.1 = ((bf16[4,32,4096]{2,1,0:T(8,128)(2,1)}), bf16[4,32,4096]{2,1,0:T(8,128)(2,1)S(1)}, u32[]{:S(2)}, u32[]{:S(2)}) async-start(bf16[4,32,4096]{2,1,0:T(8,128)(2,1)} %broadcast_in_dim.15), calls=%async_computation.1 | async-start | bytes 2097152 | tf_op jit(solution)/shard_map/all_to_all | solution.py:263
  22.4 0.0 copy-start
  22.4 0.0 copy-start.1
  22.4 0.0 copy-start.2
  22.4 0.0 copy-start.3
  22.4 1.0 %dense_tiles.3.dense_hbm = bf16[2,4,1024,1024]{3,2,1,0:T(8,128)(2,1)} custom-call(s32[2,16]{1,0:T(2,128)} %near_ref.1, f32[2,2048]{1,0:T(2,128)} %row_hbm.3, f32[2,65536]{1,0:T(2,128)} %col_hbm.3, bf16[2,4,1024,1024]{3,2,1,0:T(8,128)(2,1)} %dense_tiles.2.refs_0_), custom_call_target="tpu_custom_call", output_to_operand_aliasing={{}: (3, {})} | custom-call | flops 10000000 | bytes 8000000 | tf_op jit(solution)/shard_map/dense_tiles/pallas_call | solution.py:130
  23.4 11.1 %all-to-all-done.1 = bf16[4,32,4096]{2,1,0:T(8,128)(2,1)S(1)} async-done(((bf16[4,32,4096]{2,1,0:T(8,128)(2,1)}), bf16[4,32,4096]{2,1,0:T(8,128)(2,1)S(1)}, u32[]{:S(2)}, u32[]{:S(2)}) %all-to-all-start.1) | async-done | bytes 1048608 | tf_op jit(solution)/shard_map/all_to_all | solution.py:263
  34.5 0.0 copy-done
  34.5 0.0 copy-done.1
  34.5 0.0 copy-done.2
  34.5 0.0 copy-done.3
  34.5 1.5 %apply_tiles.1 = (f32[64,2048]{1,0:T(8,128)S(1)}, f32[64,2048]{1,0:T(8,128)S(1)}) custom-call(s32[2,16]{1,0:T(2,128)S(1)} %copy-done.2, s32[2,4]{1,0:T(2,128)S(1)} %copy-done.3, bf16[128,4096]{1,0:T(8,128)(2,1)S(1)} %bitcast.3, bf16[2,4,64,1024]{3,2,1,0:T(8,128)(2,1)S(1)} %bitcast.4, bf16[2,4,64,1024]{3,2,1,0:T(8,128)(2,1)S(1)} %bitcast.5, ...), custom_call_target="tpu_custom_call" | custom-call | flops 1000000000 | bytes 16000000 | tf_op jit(solution)/shard_map/apply_tiles/pallas_call | solution.py:216
  36.0 1.9 %collective-permute-start = (f32[64,2048]{1,0:T(8,128)S(1)}, f32[64,2048]{1,0:T(8,128)S(1)}, u32[]{:S(2)}, u32[]{:S(2)}) collective-permute-start(f32[64,2048]{1,0:T(8,128)S(1)} %get-tuple-element.14), channel_id=1, source_target_pairs={{0,1},{1,0},{2,3},{3,2},{4,5},{5,4},{6,7},{7,6},{8,9},{9,8},{10,11... | collective-permute-start | bytes 1572872 | tf_op jit(solution)/shard_map/ppermute | solution.py:268
  38.0 1.9 %collective-permute-done.other_ref = f32[64,2048]{1,0:T(8,128)S(1)} collective-permute-done((f32[64,2048]{1,0:T(8,128)S(1)}, f32[64,2048]{1,0:T(8,128)S(1)}, u32[]{:S(2)}, u32[]{:S(2)}) %collective-permute-start) | collective-permute-done | bytes 524320 | tf_op jit(solution)/shard_map/ppermute | solution.py:268
  39.8 0.2 fold.1
  40.0 27.5 %all_to_all.15 = bf16[8,8,2048]{2,1,0:T(8,128)(2,1)S(1)} all-to-all(bf16[8,8,2048]{2,1,0:T(8,128)(2,1)S(1)} %fold.1), channel_id=1, replica_groups={{0,6,12,2,8,14,4,10},{16,22,28,18,24,30,20,26},{32,38,44,34,40,46,36,42..., dimensions={0} | all-to-all | bytes 524288 | tf_op jit(solution)/shard_map/all_to_all | solution.py:275
  67.5 0.7 convert_reduce_fusion
Async XLA Ops:
  1.5 14.2 %all-to-all-start = ((bf16[8,4,4096]{2,1,0:T(4,128)(2,1)}), bf16[8,4,4096]{2,1,0:T(4,128)(2,1)S(1)}, u32[]{:S(2)}, u32[]{:S(2)}) async-start(bf16[8,4,4096]{2,1,0:T(4,128)(2,1)} %broadcast_in_dim.6), calls=%async_computation | async-start | bytes 524288 | tf_op jit(solution)/shard_map/all_to_all | solution.py:258
  16.9 17.6 %all-to-all-start.1 = ((bf16[4,32,4096]{2,1,0:T(8,128)(2,1)}), bf16[4,32,4096]{2,1,0:T(8,128)(2,1)S(1)}, u32[]{:S(2)}, u32[]{:S(2)}) async-start(bf16[4,32,4096]{2,1,0:T(8,128)(2,1)} %broadcast_in_dim.15), calls=%async_computation.1 | async-start | bytes 2097152 | tf_op jit(solution)/shard_map/all_to_all | solution.py:263
  22.4 12.1 %copy-start = (bf16[2,4,1024,64]{2,3,1,0:T(8,128)(2,1)S(1)}, bf16[2,4,1024,64]{2,3,1,0:T(8,128)(2,1)}, u32[]{:S(2)}) copy-start(bf16[2,4,1024,64]{2,3,1,0:T(8,128)(2,1)} %param.9) | copy-start | bytes 3145732
  22.4 12.1 %copy-start.1 = (bf16[2,4,1024,64]{2,3,1,0:T(8,128)(2,1)S(1)}, bf16[2,4,1024,64]{2,3,1,0:T(8,128)(2,1)}, u32[]{:S(2)}) copy-start(bf16[2,4,1024,64]{2,3,1,0:T(8,128)(2,1)} %param.8) | copy-start | bytes 3145732
  22.4 12.1 %copy-start.2 = (s32[2,16]{1,0:T(2,128)S(1)}, s32[2,16]{1,0:T(2,128)}, u32[]{:S(2)}) copy-start(s32[2,16]{1,0:T(2,128)} %near_ref.1) | copy-start | bytes 388
  22.4 12.1 %copy-start.3 = (s32[2,4]{1,0:T(2,128)S(1)}, s32[2,4]{1,0:T(2,128)}, u32[]{:S(2)}) copy-start(s32[2,4]{1,0:T(2,128)} %ranks_ref.1) | copy-start | bytes 100
  36.0 3.8 %collective-permute-start = (f32[64,2048]{1,0:T(8,128)S(1)}, f32[64,2048]{1,0:T(8,128)S(1)}, u32[]{:S(2)}, u32[]{:S(2)}) collective-permute-start(f32[64,2048]{1,0:T(8,128)S(1)} %get-tuple-element.14), channel_id=1, source_target_pairs={{0,1},{1,0},{2,3},{3,2},{4,5},{5,4},{6,7},{7,6},{8,9},{9,8},{10,11... | collective-permute-start | bytes 1572872 | tf_op jit(solution)/shard_map/ppermute | solution.py:268
